TPU v7x, 32 devices: a whole 2x2x4 slice. The times are simulated.
32 devices in a mesh: ctx: 8 (over z, y), fsdp: 4 (over x, core).
Axes of the slice: x: 2, y: 2, z: 4, core: 2. Of those that a mesh axis runs over, the one named last changes fastest.
Arguments:
- tokens: bfloat16 [4, 4096, 1024], P('fsdp', 'ctx'), may hold values from -6 to 6
- block_pos: int32 [4, 16], P('fsdp'), may hold values from 0 to 15, each once within a row
- gain_attn: bfloat16 [1024], P('fsdp'), may hold values from 0.25 to 1.75
- w_query: bfloat16 [1024, 256], P('fsdp'), may hold values from -0.1875 to 0.1875
- w_key: bfloat16 [1024, 256], P('fsdp'), may hold values from -0.1875 to 0.1875
- w_value: bfloat16 [1024, 1024], P('fsdp'), may hold values from -0.1875 to 0.1875
- w_out: bfloat16 [1024, 1024], P('fsdp'), may hold values from -2 to 2
- gain_ffn: bfloat16 [1024], P('fsdp'), may hold values from 0.25 to 1.75
- w_gate: bfloat16 [1024, 2752], P('fsdp'), may hold values from -0.1875 to 0.1875
- w_up: bfloat16 [1024, 2752], P('fsdp'), may hold values from -0.1875 to 0.1875
- w_down: bfloat16 [2752, 1024], P('fsdp'), may hold values from -0.109375 to 0.109375
- cotangent: bfloat16 [4, 4096, 1024], P('fsdp', 'ctx'), may hold values from -6 to 6
Outputs:
- output: bfloat16 [4, 4096, 1024], P('fsdp', 'ctx')
- grad_tokens: float32 [4, 4096, 1024], P('fsdp', 'ctx')
- grad_gain_attn: float32 [1024], P('fsdp')
- grad_query: float32 [1024, 256], P('fsdp')
- grad_key: float32 [1024, 256], P('fsdp')
- grad_value: float32 [1024, 1024], P('fsdp')
- grad_out: float32 [1024, 1024], P('fsdp')
- grad_gain_ffn: float32 [1024], P('fsdp')
- grad_gate: float32 [1024, 2752], P('fsdp')
- grad_up: float32 [1024, 2752], P('fsdp')
- grad_down: float32 [2752, 1024], P('fsdp')
Inputs may be any that keep to these rules, and one draw needn't show every extreme that they name: `block_pos`: each row is a permutation of the 16 position blocks of one sequence.
All inputs are finite; a program needn't handle non-finite values.
Results may differ from a plain program's by a relative error of at most 0.015.
Values may be sent and summed in bfloat16 or wider, within the bound.
A program may use at most 512 MiB of HBM per device.

v0:
```python
import jax
import jax.numpy as jnp
from jax import lax
from jax.sharding import PartitionSpec as P

HEADS = 16
FDIM = 16
VDIM = 64
BLOCK = 256
highest = lax.Precision.HIGHEST
eps_norm = 1e-05
root_half = 0.7071067811865476


def features(scaled):
    outer_prod = scaled[..., :, None] * scaled[..., None, :]
    flattened = (
        outer_prod.reshape(scaled.shape[:-1] + (scaled.shape[-1] * scaled.shape[-1],)) * root_half
    )
    constant = jnp.ones(scaled.shape[:-1] + (1,), jnp.float32)
    return jnp.concatenate([constant, scaled, flattened], axis=-1)


def features_back(scaled, grad_feat):
    feat_dim = scaled.shape[-1]
    linear = grad_feat[..., 1 : 1 + feat_dim]
    square = (
        grad_feat[..., 1 + feat_dim :].reshape(scaled.shape[:-1] + (feat_dim, feat_dim)) * root_half
    )
    return linear + jnp.einsum("...ab,...b->...a", square + jnp.swapaxes(square, -1, -2), scaled)


def norm_forward(values, gain_vector):
    inv_rms = lax.rsqrt(jnp.mean(values * values, axis=-1, keepdims=True) + eps_norm)
    return (values * inv_rms * gain_vector, inv_rms)


def norm_backward(values, inv_rms, gain_vector, grad_normed):
    weighted = grad_normed * gain_vector
    grad_gain = jnp.sum(grad_normed * values * inv_rms, axis=0)
    grad_values = inv_rms * weighted - values * (inv_rms * inv_rms * inv_rms) * jnp.mean(
        weighted * values, axis=-1, keepdims=True
    )
    return (grad_values, grad_gain)


def block_group():
    for group_size in (8, 4, 2):
        return group_size
    return 1


def body(
    tokens,
    block_pos,
    gain_attn,
    w_query,
    w_key,
    w_value,
    w_out,
    gain_ffn,
    w_gate,
    w_up,
    w_down,
    cotangent,
):
    gathered = (
        lax.all_gather(gain_attn, "fsdp", axis=0, tiled=True),
        lax.all_gather(w_query, "fsdp", axis=0, tiled=True),
        lax.all_gather(w_key, "fsdp", axis=0, tiled=True),
        lax.all_gather(w_value, "fsdp", axis=0, tiled=True),
        lax.all_gather(w_out, "fsdp", axis=0, tiled=True),
        lax.all_gather(gain_ffn, "fsdp", axis=0, tiled=True),
        lax.all_gather(w_gate, "fsdp", axis=0, tiled=True),
        lax.all_gather(w_up, "fsdp", axis=0, tiled=True),
        lax.all_gather(w_down, "fsdp", axis=0, tiled=True),
    )
    norm_one_gain = gathered[0].astype(jnp.float32)
    query_full, key_full, value_full, out_full = (
        gathered[1],
        gathered[2],
        gathered[3],
        gathered[4],
    )
    norm_two_gain = gathered[5].astype(jnp.float32)
    gate_full, up_full, down_full = (gathered[6], gathered[7], gathered[8])
    residual = tokens[0].astype(jnp.float32)
    row_count = residual.shape[0]
    local_blocks = row_count // BLOCK
    feat_width = 1 + FDIM + FDIM * FDIM
    positions = block_pos[0]
    own_positions = lax.dynamic_slice_in_dim(
        positions, lax.axis_index("ctx") * local_blocks, local_blocks
    )
    normed_one, inv_rms_one = norm_forward(residual, norm_one_gain)
    normed_one_low = normed_one.astype(jnp.bfloat16)
    queries = jnp.dot(normed_one_low, query_full, preferred_element_type=jnp.float32).astype(
        jnp.bfloat16
    )
    keys_all = jnp.dot(normed_one_low, key_full, preferred_element_type=jnp.float32).astype(
        jnp.bfloat16
    )
    values_all = jnp.dot(normed_one_low, value_full, preferred_element_type=jnp.float32).astype(
        jnp.bfloat16
    )
    query_blocks = queries.reshape(local_blocks, BLOCK, HEADS, FDIM)
    key_blocks = keys_all.reshape(local_blocks, BLOCK, HEADS, FDIM)
    value_blocks = values_all.reshape(local_blocks, BLOCK, HEADS, VDIM)
    query_scaled = query_blocks.astype(jnp.float32) * 0.5
    key_scaled = key_blocks.astype(jnp.float32) * 0.5
    phi_query = features(query_scaled).astype(jnp.bfloat16)
    phi_key = features(key_scaled).astype(jnp.bfloat16)
    state_zero = jnp.zeros((local_blocks, HEADS, feat_width, VDIM), jnp.float32)
    norm_zero = jnp.zeros((local_blocks, HEADS, feat_width), jnp.float32)
    running = (state_zero, norm_zero)
    key_piece = lax.all_gather(keys_all, "ctx", axis=0, tiled=True)
    value_piece = lax.all_gather(values_all, "ctx", axis=0, tiled=True)
    block_count = key_piece.shape[0] // BLOCK
    group_size = block_group()
    others = positions
    key_groups = key_piece.reshape(block_count // group_size, group_size, BLOCK, HEADS, FDIM)
    value_groups = value_piece.reshape(block_count // group_size, group_size, BLOCK, HEADS, VDIM)
    other_groups = others.reshape(block_count // group_size, group_size)

    def one_group(inner_sum, group_args):
        keys_here, values_here, places = group_args
        key_feat = features(keys_here.astype(jnp.float32) * 0.5).astype(jnp.bfloat16)
        states = jnp.einsum(
            "gthf,gthv->ghfv", key_feat, values_here, preferred_element_type=jnp.float32
        )
        norm_sums = jnp.sum(key_feat.astype(jnp.float32), axis=1)
        earlier = (places[None, :] < own_positions[:, None]).astype(jnp.float32)
        return (
            (
                inner_sum[0] + jnp.einsum("ig,ghfv->ihfv", earlier, states, precision=highest),
                inner_sum[1] + jnp.einsum("ig,ghf->ihf", earlier, norm_sums, precision=highest),
            ),
            None,
        )

    running, unused = lax.scan(one_group, running, (key_groups, value_groups, other_groups))
    prefix, prefix_norm = running
    phi_query_wide = phi_query.astype(jnp.float32)
    scores = (
        jnp.einsum("nshf,nthf->nhst", query_blocks, key_blocks, preferred_element_type=jnp.float32)
        * 0.25
    )
    kernel = 1.0 + scores + 0.5 * scores * scores
    kernel_low = kernel.astype(jnp.bfloat16)
    numerator = jnp.einsum(
        "nhst,nthv->nshv", kernel_low, value_blocks, preferred_element_type=jnp.float32
    ) + jnp.einsum("nshf,nhfv->nshv", phi_query_wide, prefix, precision=highest)
    denominator = jnp.transpose(jnp.sum(kernel, axis=-1), (0, 2, 1)) + jnp.einsum(
        "nshf,nhf->nsh", phi_query_wide, prefix_norm, precision=highest
    )
    attention_full = numerator / denominator[..., None]
    attention_low = attention_full.reshape(row_count, HEADS * VDIM).astype(jnp.bfloat16)
    middle = residual + jnp.dot(attention_low, out_full, preferred_element_type=jnp.float32)
    normed_two, inv_rms_two = norm_forward(middle, norm_two_gain)
    normed_two_low = normed_two.astype(jnp.bfloat16)
    gate_pre = jnp.dot(normed_two_low, gate_full, preferred_element_type=jnp.float32)
    up_pre = jnp.dot(normed_two_low, up_full, preferred_element_type=jnp.float32)
    sigmoid_gate = jax.nn.sigmoid(gate_pre)
    silu_gate = gate_pre * sigmoid_gate
    hidden_low = (silu_gate * up_pre).astype(jnp.bfloat16)
    result = middle + jnp.dot(hidden_low, down_full, preferred_element_type=jnp.float32)
    output = result.astype(jnp.bfloat16)[None]
    cotangent_low = cotangent[0]
    grad_out_full = cotangent_low.astype(jnp.float32)
    grad_down_full = jnp.einsum(
        "tf,td->fd", hidden_low, cotangent_low, preferred_element_type=jnp.float32
    )
    grad_hidden = jnp.einsum(
        "td,fd->tf", cotangent_low, down_full, preferred_element_type=jnp.float32
    )
    grad_gate_pre = (
        grad_hidden * up_pre * (sigmoid_gate * (1.0 + gate_pre * (1.0 - sigmoid_gate)))
    ).astype(jnp.bfloat16)
    grad_up_pre = (grad_hidden * silu_gate).astype(jnp.bfloat16)
    grad_gate_full = jnp.einsum(
        "td,tf->df", normed_two_low, grad_gate_pre, preferred_element_type=jnp.float32
    )
    grad_up_full = jnp.einsum(
        "td,tf->df", normed_two_low, grad_up_pre, preferred_element_type=jnp.float32
    )
    grad_normed_two = jnp.einsum(
        "tf,df->td", grad_gate_pre, gate_full, preferred_element_type=jnp.float32
    ) + jnp.einsum("tf,df->td", grad_up_pre, up_full, preferred_element_type=jnp.float32)
    grad_middle_norm, grad_gain_two = norm_backward(
        middle, inv_rms_two, norm_two_gain, grad_normed_two
    )
    grad_middle = grad_out_full + grad_middle_norm
    grad_branch = grad_middle.astype(jnp.bfloat16)
    grad_out_proj = jnp.einsum(
        "ta,td->ad", attention_low, grad_branch, preferred_element_type=jnp.float32
    )
    grad_attention = jnp.einsum(
        "td,ad->ta", grad_branch, out_full, preferred_element_type=jnp.float32
    )
    grad_attention = grad_attention.reshape(local_blocks, BLOCK, HEADS, VDIM)
    grad_numerator = (grad_attention / denominator[..., None]).astype(jnp.bfloat16)
    grad_denominator = (-jnp.sum(grad_attention * attention_full, axis=-1) / denominator).astype(
        jnp.bfloat16
    )
    grad_denom_wide = grad_denominator.astype(jnp.float32)
    grad_kernel = (
        jnp.einsum(
            "nshv,nthv->nhst", grad_numerator, value_blocks, preferred_element_type=jnp.float32
        )
        + jnp.transpose(grad_denom_wide, (0, 2, 1))[..., None]
    )
    grad_scores = ((1.0 + scores) * grad_kernel).astype(jnp.bfloat16)
    flat_numer = grad_numerator.reshape(row_count, HEADS * VDIM)
    flat_denom = grad_denominator.reshape(row_count, HEADS)
    running = (state_zero, norm_zero)
    query_piece = lax.all_gather(queries, "ctx", axis=0, tiled=True)
    numer_piece = lax.all_gather(flat_numer, "ctx", axis=0, tiled=True)
    denom_piece = lax.all_gather(flat_denom, "ctx", axis=0, tiled=True)
    block_count = query_piece.shape[0] // BLOCK
    group_size = block_group()
    others = positions
    query_groups = query_piece.reshape(block_count // group_size, group_size, BLOCK, HEADS, FDIM)
    numer_groups = numer_piece.reshape(block_count // group_size, group_size, BLOCK, HEADS, VDIM)
    denom_groups = denom_piece.reshape(block_count // group_size, group_size, BLOCK, HEADS)
    other_groups = others.reshape(block_count // group_size, group_size)

    def one_group(inner_sum, group_args):
        queries_here, numer_here, denom_here, places = group_args
        query_feat = features(queries_here.astype(jnp.float32) * 0.5).astype(jnp.bfloat16)
        grad_states = jnp.einsum(
            "gthf,gthv->ghfv", query_feat, numer_here, preferred_element_type=jnp.float32
        )
        grad_norms = jnp.einsum(
            "gthf,gth->ghf", query_feat, denom_here, preferred_element_type=jnp.float32
        )
        later_mask = (places[None, :] > own_positions[:, None]).astype(jnp.float32)
        return (
            (
                inner_sum[0]
                + jnp.einsum("ig,ghfv->ihfv", later_mask, grad_states, precision=highest),
                inner_sum[1] + jnp.einsum("ig,ghf->ihf", later_mask, grad_norms, precision=highest),
            ),
            None,
        )

    running, unused = lax.scan(
        one_group, running, (query_groups, numer_groups, denom_groups, other_groups)
    )
    later_states, later_norms = running
    grad_phi_query = (
        jnp.einsum("nshv,nhfv->nshf", grad_numerator.astype(jnp.float32), prefix, precision=highest)
        + grad_denom_wide[..., None] * prefix_norm[:, None, :, :]
    )
    grad_phi_key = (
        jnp.einsum(
            "nthv,nhfv->nthf", value_blocks.astype(jnp.float32), later_states, precision=highest
        )
        + later_norms[:, None, :, :]
    )
    grad_values = jnp.einsum(
        "nhst,nshv->nthv", kernel_low, grad_numerator, preferred_element_type=jnp.float32
    ) + jnp.einsum("nthf,nhfv->nthv", phi_key.astype(jnp.float32), later_states, precision=highest)
    grad_values_low = grad_values.reshape(row_count, HEADS * VDIM).astype(jnp.bfloat16)
    grad_queries = jnp.einsum(
        "nhst,nthf->nshf", grad_scores, key_blocks, preferred_element_type=jnp.float32
    ) * 0.25 + 0.5 * features_back(query_scaled, grad_phi_query)
    grad_queries_low = grad_queries.reshape(row_count, HEADS * FDIM).astype(jnp.bfloat16)
    grad_keys = jnp.einsum(
        "nhst,nshf->nthf", grad_scores, query_blocks, preferred_element_type=jnp.float32
    ) * 0.25 + 0.5 * features_back(key_scaled, grad_phi_key)
    grad_keys_low = grad_keys.reshape(row_count, HEADS * FDIM).astype(jnp.bfloat16)
    grad_query_full = jnp.einsum(
        "td,tk->dk", normed_one_low, grad_queries_low, preferred_element_type=jnp.float32
    )
    grad_key_full = jnp.einsum(
        "td,tk->dk", normed_one_low, grad_keys_low, preferred_element_type=jnp.float32
    )
    grad_value_full = jnp.einsum(
        "td,tk->dk", normed_one_low, grad_values_low, preferred_element_type=jnp.float32
    )
    grad_normed_one = (
        jnp.einsum("tk,dk->td", grad_queries_low, query_full, preferred_element_type=jnp.float32)
        + jnp.einsum("tk,dk->td", grad_keys_low, key_full, preferred_element_type=jnp.float32)
        + jnp.einsum("tk,dk->td", grad_values_low, value_full, preferred_element_type=jnp.float32)
    )
    grad_from_norm, grad_gain_one = norm_backward(
        residual, inv_rms_one, norm_one_gain, grad_normed_one
    )
    grad_tokens = (grad_middle + grad_from_norm)[None]
    shards = (
        lax.psum_scatter(
            grad_gain_one.astype(jnp.bfloat16), "fsdp", scatter_dimension=0, tiled=True
        ).astype(jnp.float32),
        lax.psum_scatter(
            grad_query_full.astype(jnp.bfloat16), "fsdp", scatter_dimension=0, tiled=True
        ).astype(jnp.float32),
        lax.psum_scatter(
            grad_key_full.astype(jnp.bfloat16), "fsdp", scatter_dimension=0, tiled=True
        ).astype(jnp.float32),
        lax.psum_scatter(
            grad_value_full.astype(jnp.bfloat16), "fsdp", scatter_dimension=0, tiled=True
        ).astype(jnp.float32),
        lax.psum_scatter(
            grad_out_proj.astype(jnp.bfloat16), "fsdp", scatter_dimension=0, tiled=True
        ).astype(jnp.float32),
        lax.psum_scatter(
            grad_gain_two.astype(jnp.bfloat16), "fsdp", scatter_dimension=0, tiled=True
        ).astype(jnp.float32),
        lax.psum_scatter(
            grad_gate_full.astype(jnp.bfloat16), "fsdp", scatter_dimension=0, tiled=True
        ).astype(jnp.float32),
        lax.psum_scatter(
            grad_up_full.astype(jnp.bfloat16), "fsdp", scatter_dimension=0, tiled=True
        ).astype(jnp.float32),
        lax.psum_scatter(
            grad_down_full.astype(jnp.bfloat16), "fsdp", scatter_dimension=0, tiled=True
        ).astype(jnp.float32),
    )
    totals = lax.psum(
        (
            shards[0],
            shards[1],
            shards[2],
            shards[3],
            shards[4],
            shards[5],
            shards[6],
            shards[7],
            shards[8],
        ),
        "ctx",
    )
    return (
        output,
        grad_tokens,
        totals[0],
        totals[1],
        totals[2],
        totals[3],
        totals[4],
        totals[5],
        totals[6],
        totals[7],
        totals[8],
    )


def solution(mesh):
    in_specs = (
        P("fsdp", "ctx", None),
        P("fsdp", None),
        P("fsdp"),
        P("fsdp", None),
        P("fsdp", None),
        P("fsdp", None),
        P("fsdp", None),
        P("fsdp"),
        P("fsdp", None),
        P("fsdp", None),
        P("fsdp", None),
        P("fsdp", "ctx", None),
    )
    out_specs = (
        P("fsdp", "ctx", None),
        P("fsdp", "ctx", None),
        P("fsdp"),
        P("fsdp", None),
        P("fsdp", None),
        P("fsdp", None),
        P("fsdp", None),
        P("fsdp"),
        P("fsdp", None),
        P("fsdp", None),
        P("fsdp", None),
    )
    return jax.shard_map(body, mesh=mesh, in_specs=in_specs, out_specs=out_specs, check_vma=False)
```

profile of v0, /device:TPU:0, one launch (start us, length us, event | category | flops | bytes accessed | tf_op | source)
XLA Modules:
  0.0 1292.5 jit_solution(17293718670228395038)
XLA Ops:
  16.1 9.3 all_gather.45
  96.9 118.5 %all-gather.16.cloned.1.call-done = bf16[4096,1024]{1,0:T(8,128)(2,1)} async-done(((bf16[512,1024]{1,0:T(8,128)(2,1)}), bf16[4096,1024]{1,0:T(8,128)(2,1)}) %all-gather.16.cloned.1.call-update) | async-done | bytes 8388624 | tf_op jit(solution)/shard_map/all_gather | solution.py:117
  215.5 22.2 %reshape.269 = bf16[2,8,256,16,64]{4,3,2,1,0:T(8,128)(2,1)} reshape(bf16[4096,1024]{1,0:T(8,128)(2,1)} %all-gather.16.cloned.1.call-done) | data formatting | bytes 16777216 | tf_op jit(solution)/shard_map/reshape | solution.py:122
  237.7 19.7 %copy.112 = bf16[2,8,256,16,64]{2,4,3,1,0:T(8,128)(2,1)} copy(bf16[2,8,256,16,64]{4,3,2,1,0:T(8,128)(2,1)} %reshape.269) | data formatting | bytes 16777216
  257.4 111.2 %while.26 = (s32[]{:T(128)}, f32[2,16,273,64]{2,0,3,1:T(2,128)S(1)}, f32[2,16,273]{2,0,1:T(2,128)S(1)}, s32[2,8]{1,0:T(2,128)S(1)}, s32[2]{0:T(128)S(1)}, /*inde...) while((s32[]{:T(128)}, ...), condition=%wide.region_3.4_spmd.clone, body=%wide.region_1.3_spmd.clone.sunk | while | flops 1343690752 | bytes 159030480 | solution.py:141
  278.4 13.8 %fusion.184 = f32[8,16,273,64]{2,3,1,0:T(8,128)} fusion(bf16[8,256,16,256]{1,3,2,0:T(8,128)(2,1)} %bitcast.288, bf16[8,256,16,16]{1,3,2,0:T(8,128)(2,1)} %copy-done.1, bf16[273]{0:T(512)(128)(2,1)S(1)} %pad.clone.2, bf16[2,8,256,16,64]{2,4,3,1,0:T(8,128)(2,1)} %get-tuple-element.396, s32[]{:T(128)S(6)} %copy.272), kind=kOutput, calls=%fused_computation.5.clone.1 | convolution fusion | flops 1198718976 | bytes 30966310 | tf_op jit(solution)/shard_map/while/body/eval_jaxpr/gthf,gthv->ghfv/dot_general | solution.py:128
  292.3 19.9 %select_add_fusion.4 = f32[2,16,273,64]{2,0,3,1:T(2,128)S(1)} fusion(f32[2,16,273,64]{2,0,3,1:T(2,128)S(1)} %get-tuple-element.380, pred[]{:T(512)S(6)} %compare.6, f32[8,16,273,64]{2,3,1,0:T(8,128)} %fusion.184, s32[8]{0:T(128)S(1)} %fusion.185, s32[2]{0:T(128)S(1)} %get-tuple-element.394), kind=kOutput, calls=%fused_computation.9.clone.1 | convolution fusion | flops 54792208 | bytes 13418537 | tf_op jit(solution)/shard_map/while/body/eval_jaxpr/ig,ghfv->ihfv/dot_general | solution.py:135
  333.4 15.2 %fusion.184 = f32[8,16,273,64]{2,3,1,0:T(8,128)} fusion(bf16[8,256,16,256]{1,3,2,0:T(8,128)(2,1)} %bitcast.288, bf16[8,256,16,16]{1,3,2,0:T(8,128)(2,1)} %copy-done.1, bf16[273]{0:T(512)(128)(2,1)S(1)} %pad.clone.2, bf16[2,8,256,16,64]{2,4,3,1,0:T(8,128)(2,1)} %get-tuple-element.396, s32[]{:T(128)S(6)} %copy.272), kind=kOutput, calls=%fused_computation.5.clone.1 | convolution fusion | flops 1198718976 | bytes 30966310 | tf_op jit(solution)/shard_map/while/body/eval_jaxpr/gthf,gthv->ghfv/dot_general | solution.py:128
  348.6 19.3 %select_add_fusion.4 = f32[2,16,273,64]{2,0,3,1:T(2,128)S(1)} fusion(f32[2,16,273,64]{2,0,3,1:T(2,128)S(1)} %get-tuple-element.380, pred[]{:T(512)S(6)} %compare.6, f32[8,16,273,64]{2,3,1,0:T(8,128)} %fusion.184, s32[8]{0:T(128)S(1)} %fusion.185, s32[2]{0:T(128)S(1)} %get-tuple-element.394), kind=kOutput, calls=%fused_computation.9.clone.1 | convolution fusion | flops 54792208 | bytes 13418537 | tf_op jit(solution)/shard_map/while/body/eval_jaxpr/ig,ghfv->ihfv/dot_general | solution.py:135
  407.0 12.3 multiply_convert_fusion.5
  470.3 16.5 %fusion.44 = f32[2,256,16,16]{1,3,2,0:T(8,128)S(1)} fusion(f32[2,256,16,16,16]{1,4,3,2,0:T(8,128)} %bitcast.293, f32[2,256,16,16]{1,3,2,0:T(8,128)S(1)} %copy-done.21), kind=kLoop, calls=%fused_computation.67 | loop fusion | flops 6160384 | bytes 9437184 | tf_op jit(solution)/shard_map/...ab,...b->...a/dot_general | solution.py:30
  530.6 31.4 %all_gather.55 = bf16[4096,16]{0,1:T(8,128)(2,1)S(1)} all-gather(bf16[512,16]{0,1:T(8,128)(2,1)S(1)} %bitcast.321), channel_id=1, replica_groups=mesh['ctx'=8,'fsdp'=4] {'ctx'}, dimensions={0}, use_global_device_ids=true | all-gather | bytes 147456 | tf_op jit(solution)/shard_map/all_gather | solution.py:218
  569.9 22.2 %reshape.271 = bf16[2,8,256,16,64]{4,3,2,1,0:T(8,128)(2,1)} reshape(bf16[4096,1024]{1,0:T(8,128)(2,1)} %all-gather.28.cloned.1.call-done) | data formatting | bytes 16777216 | tf_op jit(solution)/shard_map/reshape | solution.py:223
  592.1 19.7 %copy.135 = bf16[2,8,256,16,64]{2,4,3,1,0:T(8,128)(2,1)} copy(bf16[2,8,256,16,64]{4,3,2,1,0:T(8,128)(2,1)} %reshape.271) | data formatting | bytes 16777216
  611.7 114.5 %while.27 = (s32[]{:T(128)}, f32[2,16,273,64]{2,0,3,1:T(2,128)S(1)}, f32[2,16,273]{2,0,1:T(2,128)S(1)}, s32[2,8]{1,0:T(2,128)S(1)}, s32[2]{0:T(128)S(1)}, /*inde...) while((s32[]{:T(128)}, ...), condition=%wide.region_9.10_spmd.clone, body=%wide.region_8.9_spmd.clone.sunk | while | flops 1352671360 | bytes 92249264 | solution.py:246
  623.3 9.2 fusion.193
  632.5 16.2 %fusion.191 = f32[8,16,273,64]{2,3,1,0:T(8,128)} fusion(bf16[8,256,16,256]{1,3,2,0:T(8,128)(2,1)} %bitcast.290, bf16[8,256,16,16]{1,3,2,0:T(8,128)(2,1)} %copy-done.9, bf16[273]{0:T(512)(128)(2,1)S(1)} %pad.3.clone.2, bf16[2,8,256,16,64]{2,4,3,1,0:T(8,128)(2,1)} %get-tuple-element.431, s32[]{:T(128)S(6)} %copy.281), kind=kOutput, calls=%fused_computation.30.clone.1 | convolution fusion | flops 1198718976 | bytes 30966310 | tf_op jit(solution)/shard_map/while/body/eval_jaxpr/gthf,gthv->ghfv/dot_general | solution.py:230
  648.8 19.8 %select_add_fusion.5 = f32[2,16,273,64]{2,0,3,1:T(2,128)S(1)} fusion(f32[2,16,273,64]{2,0,3,1:T(2,128)S(1)} %get-tuple-element.414, pred[]{:T(512)S(6)} %compare.7, f32[8,16,273,64]{2,3,1,0:T(8,128)} %fusion.191, s32[8]{0:T(128)S(1)} %fusion.192, s32[2]{0:T(128)S(1)} %get-tuple-element.429), kind=kOutput, calls=%fused_computation.35.clone.1 | convolution fusion | flops 54792208 | bytes 13418537 | tf_op jit(solution)/shard_map/while/body/eval_jaxpr/ig,ghfv->ihfv/dot_general | solution.py:240
  680.4 9.3 fusion.193
  689.7 16.1 %fusion.191 = f32[8,16,273,64]{2,3,1,0:T(8,128)} fusion(bf16[8,256,16,256]{1,3,2,0:T(8,128)(2,1)} %bitcast.290, bf16[8,256,16,16]{1,3,2,0:T(8,128)(2,1)} %copy-done.9, bf16[273]{0:T(512)(128)(2,1)S(1)} %pad.3.clone.2, bf16[2,8,256,16,64]{2,4,3,1,0:T(8,128)(2,1)} %get-tuple-element.431, s32[]{:T(128)S(6)} %copy.281), kind=kOutput, calls=%fused_computation.30.clone.1 | convolution fusion | flops 1198718976 | bytes 30966310 | tf_op jit(solution)/shard_map/while/body/eval_jaxpr/gthf,gthv->ghfv/dot_general | solution.py:230
  705.7 19.7 %select_add_fusion.5 = f32[2,16,273,64]{2,0,3,1:T(2,128)S(1)} fusion(f32[2,16,273,64]{2,0,3,1:T(2,128)S(1)} %get-tuple-element.414, pred[]{:T(512)S(6)} %compare.7, f32[8,16,273,64]{2,3,1,0:T(8,128)} %fusion.191, s32[8]{0:T(128)S(1)} %fusion.192, s32[2]{0:T(128)S(1)} %get-tuple-element.429), kind=kOutput, calls=%fused_computation.35.clone.1 | convolution fusion | flops 54792208 | bytes 13418537 | tf_op jit(solution)/shard_map/while/body/eval_jaxpr/ig,ghfv->ihfv/dot_general | solution.py:240
  739.2 17.3 %fusion.41 = f32[2,256,16,16]{1,3,2,0:T(8,128)} fusion(f32[2,256,16,16,16]{1,4,3,2,0:T(8,128)} %bitcast.294, f32[2,256,16,16]{1,3,2,0:T(8,128)S(1)} %copy-done.23), kind=kLoop, calls=%fused_computation.63 | loop fusion | flops 6160384 | bytes 9437184 | tf_op jit(solution)/shard_map/...ab,...b->...a/dot_general | solution.py:30
  820.9 34.4 %reduce-scatter.12.cloned.1.call-done = bf16[256,1024]{1,0:T(8,128)(2,1)} async-done(((bf16[1024,1024]{1,0:T(8,128)(2,1)}), bf16[256,1024]{1,0:T(8,128)(2,1)}) %reduce-scatter.12.cloned.1.call-update) | async-done | bytes 524304 | tf_op jit(solution)/shard_map/reduce_scatter | solution.py:300
  855.3 430.5 %all-reduce.5 = (f32[256]{0:T(256)}, f32[256,256]{1,0:T(8,128)}, f32[256,256]{1,0:T(8,128)}, f32[256,1024]{1,0:T(8,128)}, f32[256,1024]{1,0:T(8,128)}, /*index=5...) all-reduce(f32[256]{0:T(256)S(1)} %get-tuple-element.267, ...), channel_id=1, replica_groups=mesh['ctx'=8,'fsdp'=4] {'ctx'}, use_global_device_ids=true, to_apply=%region_13.14 | all-reduce | flops 2769408 | bytes 16617472 | tf_op jit(solution)/shard_map/psum | solution.py:319
  (326 shorter events, 362.9 us)
Async XLA Ops:
  7.2 28.8 %copy-start.11 = (bf16[1,512,1024]{2,1,0:T(8,128)(2,1)S(1)}, bf16[1,512,1024]{2,1,0:T(8,128)(2,1)}, u32[]{:S(2)}) copy-start(bf16[1,512,1024]{2,1,0:T(8,128)(2,1)} %param.16) | copy-start | bytes 3145732
  7.2 28.7 %all-gather.12.cloned.1.call-start = ((), (), s32[]{:S(2)}) async-start(), calls=%async_computation.7 | async-start | bytes 2621440 | tf_op jit(solution)/shard_map/all_gather | solution.py:71
  7.9 81.4 %all-gather.14.cloned.1.call-start = ((), (), s32[]{:S(2)}) async-start(), calls=%async_computation.8 | async-start | bytes 2359296 | tf_op jit(solution)/shard_map/all_gather | solution.py:116
  14.6 35.1 %copy-start.53 = (f32[4,1,256]{2,1,0:T(1,128)}, f32[4,1,256]{2,1,0:T(1,128)S(1)}, u32[]{:S(2)}) copy-start(f32[4,1,256]{2,1,0:T(1,128)S(1)} %convert_element_type.281) | copy-start | bytes 12292
  26.1 23.6 %copy-start.58 = (f32[512]{0:T(512)}, f32[512]{0:T(512)S(1)}, u32[]{:S(2)}) copy-start(f32[512]{0:T(512)S(1)} %get-tuple-element.253) | copy-start | bytes 6148
  28.7 186.7 %all-gather.16.cloned.1.call-start = ((), (), s32[]{:S(2)}) async-start(), calls=%async_computation.9 | async-start | bytes 9437184 | tf_op jit(solution)/shard_map/all_gather | solution.py:117
  39.8 343.9 %all-gather.18.cloned.1.call-start = ((), (), s32[]{:S(2)}) async-start(), calls=%async_computation.10 | async-start | bytes 2621440 | tf_op jit(solution)/shard_map/all_gather | solution.py:72
  40.4 349.3 %all-gather.22.cloned.1.call-start = ((), (), s32[]{:S(2)}) async-start(), calls=%async_computation.12 | async-start | bytes 7045120 | tf_op jit(solution)/shard_map/all_gather | solution.py:75
  41.0 357.3 %all-gather.20.cloned.1.call-start = ((), (), s32[]{:S(2)}) async-start(), calls=%async_computation.11 | async-start | bytes 7045120 | tf_op jit(solution)/shard_map/all_gather | solution.py:74
  41.6 365.4 %all-gather.24.cloned.1.call-start = ((), (), s32[]{:S(2)}) async-start(), calls=%async_computation.13 | async-start | bytes 7045120 | tf_op jit(solution)/shard_map/all_gather | solution.py:76
  42.3 480.5 %all-gather.26.cloned.1.call-start = ((), (), s32[]{:S(2)}) async-start(), calls=%async_computation.14 | async-start | bytes 2359296 | tf_op jit(solution)/shard_map/all_gather | solution.py:216
  51.7 518.2 %all-gather.28.cloned.1.call-start = ((), (), s32[]{:S(2)}) async-start(), calls=%async_computation.15 | async-start | bytes 9437184 | tf_op jit(solution)/shard_map/all_gather | solution.py:217
  257.3 111.2 %copy-start.64 = (bf16[273]{0:T(512)(128)(2,1)S(1)}, bf16[273]{0:T(512)(128)(2,1)}, u32[]{:S(2)}) copy-start(bf16[273]{0:T(512)(128)(2,1)} %pad.9.clone) | copy-start | bytes 1642
  444.8 348.6 %reduce-scatter.8.cloned.1.call-start = ((), (), s32[]{:S(2)}) async-start(), calls=%async_computation.16 | async-start | bytes 655360 | tf_op jit(solution)/shard_map/reduce_scatter | solution.py:294
  457.1 29.7 %copy-start.10 = (bf16[2,256,16,64]{1,3,2,0:T(8,128)(2,1)}, bf16[2,256,16,64]{1,3,2,0:T(8,128)(2,1)S(1)}, u32[]{:S(2)}) copy-start(bf16[2,256,16,64]{1,3,2,0:T(8,128)(2,1)S(1)} %get-tuple-element.246) | copy-start | bytes 3145732
  499.4 294.0 %reduce-scatter.14.cloned.1.call-start = ((), (), s32[]{:S(2)}) async-start(), calls=%async_computation.19 | async-start | bytes 2621440 | tf_op jit(solution)/shard_map/reduce_scatter | solution.py:303
  502.1 291.3 %reduce-scatter.20.cloned.1.call-start = ((), (), s32[]{:S(2)}) async-start(), calls=%async_computation.22 | async-start | bytes 7045120 | tf_op jit(solution)/shard_map/reduce_scatter | solution.py:315
  509.7 283.7 %reduce-scatter.18.cloned.1.call-start = ((), (), s32[]{:S(2)}) async-start(), calls=%async_computation.21 | async-start | bytes 7045120 | tf_op jit(solution)/shard_map/reduce_scatter | solution.py:312
  517.7 278.4 %reduce-scatter.16.cloned.1.call-start = ((), (), s32[]{:S(2)}) async-start(), calls=%async_computation.20 | async-start | bytes 7045120 | tf_op jit(solution)/shard_map/reduce_scatter | solution.py:309
  526.9 35.8 %copy-start.37 = (bf16[512,1024]{1,0:T(8,128)(2,1)S(1)}, bf16[512,1024]{1,0:T(8,128)(2,1)}, u32[]{:S(2)}) copy-start(bf16[512,1024]{1,0:T(8,128)(2,1)} %multiply_convert_fusion.8) | copy-start | bytes 3145732
  526.9 35.8 %copy-start.71 = (bf16[512,2752]{0,1:T(8,128)(2,1)S(1)}, bf16[512,2752]{0,1:T(8,128)(2,1)}, u32[]{:S(2)}) copy-start(bf16[512,2752]{0,1:T(8,128)(2,1)} %get-tuple-element.244) | copy-start | bytes 8454148
  567.6 253.3 %reduce-scatter.10.cloned.1.call-start = ((), (), s32[]{:S(2)}) async-start(), calls=%async_computation.17 | async-start | bytes 655360 | tf_op jit(solution)/shard_map/reduce_scatter | solution.py:297
  770.2 85.1 %reduce-scatter.12.cloned.1.call-start = ((), (), s32[]{:S(2)}) async-start(), calls=%async_computation.18 | async-start | bytes 2621440 | tf_op jit(solution)/shard_map/reduce_scatter | solution.py:300
  803.5 51.8 %copy-start.48 = (bf16[256,256]{1,0:T(8,128)(2,1)S(1)}, bf16[256,256]{1,0:T(8,128)(2,1)}, u32[]{:S(2)}) copy-start(bf16[256,256]{1,0:T(8,128)(2,1)} %reduce-scatter.8.cloned.1.call-done) | copy-start | bytes 393220
  (69 other events, 436.9 us)
Sparse Core Ops, SparseCore 0:
  9.6 26.2 all-gather.11
  38.6 50.6 all-gather.13
  92.0 123.4 all-gather.15
  216.9 20.7 all-gather.17
  239.1 43.3 all-gather.21
  283.9 43.3 all-gather.19
  328.9 42.6 all-gather.23
  373.7 49.2 all-gather.25
  444.9 124.8 all-gather.27
  572.2 20.0 reduce-scatter.7
  594.9 31.4 reduce-scatter.13
  628.8 54.0 reduce-scatter.19
  685.6 53.9 reduce-scatter.17
  742.1 54.0 reduce-scatter.15
  799.2 21.6 reduce-scatter.9
  823.8 31.4 reduce-scatter.11
where the time goes:
time: 1300 us; the launch traced here: 1290 us
  blocking collectives  495 us (38%)
  matrix products  317 us (24%)
  waiting for transfers between devices  184 us (14%)
  local copies, waits for them, and re-layouts  168 us (13%)
  other arithmetic  111 us (9%)
  between operations  15.6 us (1%)
    psum x1, blocking collectives, body(): lax.psum((shards[0], shards[1], shards[2], shards[3], shards[4], shards[5...  430 us
    all_gather x1, waiting for transfers between devices, body(): value_piece = lax.all_gather(values_all, 'ctx', axis=0, tiled=True)  119 us
    unnamed x156, local copies, waits for them, and re-layouts  63.5 us
    dot_general x2, matrix products, one_group(): jnp.einsum('ig,ghfv->ihfv', later_mask, grad_states, precision=highest)  39.6 us
    dot_general x2, matrix products, one_group(): jnp.einsum('ig,ghfv->ihfv', earlier, states, precision=highest)  39.2 us
    another operation x12, other arithmetic  37.8 us
    reduce_scatter x1, waiting for transfers between devices, body(): lax.psum_scatter(grad_value_full.astype(jnp.bfloat16), 'fsdp', scatter_di...  34.4 us
    dot_general x2, other arithmetic, features_back(): jnp.einsum('...ab,...b->...a', square + jnp.swapaxes(square, -1, -2), sca...  33.7 us
  transfers between devices with their start and end apart: 16, of which 7 were waited for; matrix products, arithmetic and copies ran while one was open for 44% of the time, Pallas kernels for 0%

commit v1 on v0

--- a/solution.py
+++ b/solution.py
@@ -214,8 +214,13 @@
     flat_denom = grad_denominator.reshape(row_count, HEADS)
     running = (state_zero, norm_zero)
     query_piece = lax.all_gather(queries, "ctx", axis=0, tiled=True)
-    numer_piece = lax.all_gather(flat_numer, "ctx", axis=0, tiled=True)
-    denom_piece = lax.all_gather(flat_denom, "ctx", axis=0, tiled=True)
+    numer_piece, denom_piece = jnp.split(
+        lax.all_gather(
+            jnp.concatenate([flat_numer, flat_denom], axis=1), "ctx", axis=0, tiled=True
+        ),
+        [flat_numer.shape[1]],
+        axis=1,
+    )
     block_count = query_piece.shape[0] // BLOCK
     group_size = block_group()
     others = positions

time: 1300 us -> 1340 us (1.031)
  waiting for transfers between devices: 184 us -> 227 us
  blocking collectives: 495 us -> 465 us
    all_gather x1, waiting for transfers between devices: 2.24 us -> 58 us  [body(): lax.all_gather(jnp.concatenate([flat_numer, flat_denom], axis=1), 'ctx',...]
    all_gather x1 -> x0, blocking collectives: 31.4 us -> none  [body(): denom_piece = lax.all_gather(flat_denom, 'ctx', axis=0, tiled=True)]
    unnamed x156 -> x146, local copies, waits for them, and re-layouts: 63.5 us -> 65.3 us
  transfers between devices with their start and end apart: 16 -> 16, of which waited for: 7 -> 5; matrix products, arithmetic and copies ran while one was open for 44% -> 45% of each run, Pallas kernels for 0% -> 0%
where the time goes in v1:
time: 1340 us; the launch traced here: 1320 us
  blocking collectives  465 us (35%)
  matrix products  319 us (24%)
  waiting for transfers between devices  227 us (17%)
  local copies, waits for them, and re-layouts  180 us (13%)
  other arithmetic  116 us (9%)
  between operations  15.7 us (1%)
    psum x1, blocking collectives, body(): lax.psum((shards[0], shards[1], shards[2], shards[3], shards[4], shards[5...  430 us
    all_gather x1, waiting for transfers between devices, body(): value_piece = lax.all_gather(values_all, 'ctx', axis=0, tiled=True)  119 us
    unnamed x146, local copies, waits for them, and re-layouts  65.3 us
    all_gather x1, waiting for transfers between devices, body(): lax.all_gather(jnp.concatenate([flat_numer, flat_denom], axis=1), 'ctx',...  58 us
    dot_general x2, matrix products, one_group(): jnp.einsum('ig,ghfv->ihfv', earlier, states, precision=highest)  39.2 us
    dot_general x2, matrix products, one_group(): jnp.einsum('ig,ghfv->ihfv', later_mask, grad_states, precision=highest)  38.7 us
    another operation x12, other arithmetic  37.8 us
    dot_general x2, other arithmetic, features_back(): jnp.einsum('...ab,...b->...a', square + jnp.swapaxes(square, -1, -2), sca...  35.1 us
  transfers between devices with their start and end apart: 16, of which 5 were waited for; matrix products, arithmetic and copies ran while one was open for 45% of the time, Pallas kernels for 0%

profile of v1, /device:TPU:0, one launch (start us, length us, event | category | flops | bytes accessed | tf_op | source)
XLA Modules:
  0.0 1324.2 jit_solution(12932482195734430319)
XLA Ops:
  16.1 9.3 all_gather.42
  96.9 118.5 %all-gather.16.cloned.1.call-done = bf16[4096,1024]{1,0:T(8,128)(2,1)} async-done(((bf16[512,1024]{1,0:T(8,128)(2,1)}), bf16[4096,1024]{1,0:T(8,128)(2,1)}) %all-gather.16.cloned.1.call-update) | async-done | bytes 8388624 | tf_op jit(solution)/shard_map/all_gather | solution.py:117
  215.5 22.2 %reshape.269 = bf16[2,8,256,16,64]{4,3,2,1,0:T(8,128)(2,1)} reshape(bf16[4096,1024]{1,0:T(8,128)(2,1)} %all-gather.16.cloned.1.call-done) | data formatting | bytes 16777216 | tf_op jit(solution)/shard_map/reshape | solution.py:122
  237.6 19.7 %copy.112 = bf16[2,8,256,16,64]{2,4,3,1,0:T(8,128)(2,1)} copy(bf16[2,8,256,16,64]{4,3,2,1,0:T(8,128)(2,1)} %reshape.269) | data formatting | bytes 16777216
  257.3 111.0 %while.26 = (s32[]{:T(128)}, f32[2,16,273,64]{2,0,3,1:T(2,128)S(1)}, f32[2,16,273]{2,0,1:T(2,128)S(1)}, s32[2,8]{1,0:T(2,128)S(1)}, s32[2]{0:T(128)S(1)}, /*inde...) while((s32[]{:T(128)}, ...), condition=%wide.region_3.4_spmd.clone, body=%wide.region_1.3_spmd.clone.sunk | while | flops 1343690752 | bytes 159030480 | solution.py:141
  278.4 13.8 %fusion.184 = f32[8,16,273,64]{2,3,1,0:T(8,128)} fusion(bf16[8,256,16,256]{1,3,2,0:T(8,128)(2,1)} %bitcast.282, bf16[8,256,16,16]{1,3,2,0:T(8,128)(2,1)} %copy-done.1, bf16[273]{0:T(512)(128)(2,1)S(1)} %pad.clone.2, bf16[2,8,256,16,64]{2,4,3,1,0:T(8,128)(2,1)} %get-tuple-element.396, s32[]{:T(128)S(6)} %copy.265), kind=kOutput, calls=%fused_computation.5.clone.1 | convolution fusion | flops 1198718976 | bytes 30966310 | tf_op jit(solution)/shard_map/while/body/eval_jaxpr/gthf,gthv->ghfv/dot_general | solution.py:128
  292.2 19.9 %select_add_fusion.4 = f32[2,16,273,64]{2,0,3,1:T(2,128)S(1)} fusion(f32[2,16,273,64]{2,0,3,1:T(2,128)S(1)} %get-tuple-element.380, pred[]{:T(512)S(6)} %compare.6, f32[8,16,273,64]{2,3,1,0:T(8,128)} %fusion.184, s32[8]{0:T(128)S(1)} %fusion.185, s32[2]{0:T(128)S(1)} %get-tuple-element.394), kind=kOutput, calls=%fused_computation.9.clone.1 | convolution fusion | flops 54792208 | bytes 13418537 | tf_op jit(solution)/shard_map/while/body/eval_jaxpr/ig,ghfv->ihfv/dot_general | solution.py:135
  333.4 15.1 %fusion.184 = f32[8,16,273,64]{2,3,1,0:T(8,128)} fusion(bf16[8,256,16,256]{1,3,2,0:T(8,128)(2,1)} %bitcast.282, bf16[8,256,16,16]{1,3,2,0:T(8,128)(2,1)} %copy-done.1, bf16[273]{0:T(512)(128)(2,1)S(1)} %pad.clone.2, bf16[2,8,256,16,64]{2,4,3,1,0:T(8,128)(2,1)} %get-tuple-element.396, s32[]{:T(128)S(6)} %copy.265), kind=kOutput, calls=%fused_computation.5.clone.1 | convolution fusion | flops 1198718976 | bytes 30966310 | tf_op jit(solution)/shard_map/while/body/eval_jaxpr/gthf,gthv->ghfv/dot_general | solution.py:128
  348.5 19.3 %select_add_fusion.4 = f32[2,16,273,64]{2,0,3,1:T(2,128)S(1)} fusion(f32[2,16,273,64]{2,0,3,1:T(2,128)S(1)} %get-tuple-element.380, pred[]{:T(512)S(6)} %compare.6, f32[8,16,273,64]{2,3,1,0:T(8,128)} %fusion.184, s32[8]{0:T(128)S(1)} %fusion.185, s32[2]{0:T(128)S(1)} %get-tuple-element.394), kind=kOutput, calls=%fused_computation.9.clone.1 | convolution fusion | flops 54792208 | bytes 13418537 | tf_op jit(solution)/shard_map/while/body/eval_jaxpr/ig,ghfv->ihfv/dot_general | solution.py:135
  422.7 11.7 multiply_convert_fusion.5
  478.2 16.8 %fusion.44 = f32[2,256,16,16]{1,3,2,0:T(8,128)S(1)} fusion(f32[2,256,16,16,16]{1,4,3,2,0:T(8,128)} %bitcast.285, f32[2,256,16,16]{1,3,2,0:T(8,128)S(1)} %copy-done.19), kind=kLoop, calls=%fused_computation.66 | loop fusion | flops 6160384 | bytes 9437184 | tf_op jit(solution)/shard_map/...ab,...b->...a/dot_general | solution.py:30
  543.5 58.0 %all-gather.28.cloned.1.call-done = bf16[4096,1040]{1,0:T(8,128)(2,1)} async-done(((bf16[512,1040]{1,0:T(8,128)(2,1)}), bf16[4096,1040]{1,0:T(8,128)(2,1)}) %all-gather.28.cloned.1.call-update) | async-done | bytes 8519696 | tf_op jit(solution)/shard_map/all_gather | solution.py:218
  613.8 22.2 %reshape.271 = bf16[2,8,256,16,64]{4,3,2,1,0:T(8,128)(2,1)} reshape(bf16[4096,1024]{1,0:T(8,128)(2,1)} %split.8) | data formatting | bytes 16777216 | tf_op jit(solution)/shard_map/reshape | solution.py:228
  636.0 19.4 %copy.135 = bf16[2,8,256,16,64]{2,4,3,1,0:T(8,128)(2,1)} copy(bf16[2,8,256,16,64]{4,3,2,1,0:T(8,128)(2,1)} %reshape.271) | data formatting | bytes 16777216
  655.4 112.3 %while.27 = (s32[]{:T(128)}, f32[2,16,273,64]{2,0,3,1:T(2,128)S(1)}, f32[2,16,273]{2,0,1:T(2,128)S(1)}, s32[2,8]{1,0:T(2,128)S(1)}, s32[2]{0:T(128)S(1)}, /*inde...) while((s32[]{:T(128)}, ...), condition=%wide.region_9.10_spmd.clone, body=%wide.region_8.9_spmd.clone.sunk | while | flops 1352671360 | bytes 92118192 | solution.py:251
  667.2 10.8 fusion.193
  677.9 14.3 %fusion.191 = f32[8,16,273,64]{2,3,1,0:T(8,128)} fusion(bf16[8,256,16,256]{1,3,2,0:T(8,128)(2,1)} %bitcast.284, bf16[8,256,16,16]{1,3,2,0:T(8,128)(2,1)} %copy-done.8, bf16[273]{0:T(512)(128)(2,1)S(1)} %pad.3.clone.2, bf16[2,8,256,16,64]{2,4,3,1,0:T(8,128)(2,1)} %get-tuple-element.431, s32[]{:T(128)S(6)} %copy.274), kind=kOutput, calls=%fused_computation.30.clone.1 | convolution fusion | flops 1198718976 | bytes 30966310 | tf_op jit(solution)/shard_map/while/body/eval_jaxpr/gthf,gthv->ghfv/dot_general | solution.py:235
  692.2 19.3 %select_add_fusion.5 = f32[2,16,273,64]{2,0,3,1:T(2,128)S(1)} fusion(f32[2,16,273,64]{2,0,3,1:T(2,128)S(1)} %get-tuple-element.414, pred[]{:T(512)S(6)} %compare.7, f32[8,16,273,64]{2,3,1,0:T(8,128)} %fusion.191, s32[8]{0:T(128)S(1)} %fusion.192, s32[2]{0:T(128)S(1)} %get-tuple-element.429), kind=kOutput, calls=%fused_computation.35.clone.1 | convolution fusion | flops 54792208 | bytes 13418537 | tf_op jit(solution)/shard_map/while/body/eval_jaxpr/ig,ghfv->ihfv/dot_general | solution.py:245
  723.2 10.6 fusion.193
  733.8 14.2 %fusion.191 = f32[8,16,273,64]{2,3,1,0:T(8,128)} fusion(bf16[8,256,16,256]{1,3,2,0:T(8,128)(2,1)} %bitcast.284, bf16[8,256,16,16]{1,3,2,0:T(8,128)(2,1)} %copy-done.8, bf16[273]{0:T(512)(128)(2,1)S(1)} %pad.3.clone.2, bf16[2,8,256,16,64]{2,4,3,1,0:T(8,128)(2,1)} %get-tuple-element.431, s32[]{:T(128)S(6)} %copy.274), kind=kOutput, calls=%fused_computation.30.clone.1 | convolution fusion | flops 1198718976 | bytes 30966310 | tf_op jit(solution)/shard_map/while/body/eval_jaxpr/gthf,gthv->ghfv/dot_general | solution.py:235
  747.9 19.4 %select_add_fusion.5 = f32[2,16,273,64]{2,0,3,1:T(2,128)S(1)} fusion(f32[2,16,273,64]{2,0,3,1:T(2,128)S(1)} %get-tuple-element.414, pred[]{:T(512)S(6)} %compare.7, f32[8,16,273,64]{2,3,1,0:T(8,128)} %fusion.191, s32[8]{0:T(128)S(1)} %fusion.192, s32[2]{0:T(128)S(1)} %get-tuple-element.429), kind=kOutput, calls=%fused_computation.35.clone.1 | convolution fusion | flops 54792208 | bytes 13418537 | tf_op jit(solution)/shard_map/while/body/eval_jaxpr/ig,ghfv->ihfv/dot_general | solution.py:245
  782.2 18.2 %fusion.41 = f32[2,256,16,16]{1,3,2,0:T(8,128)} fusion(f32[2,256,16,16,16]{1,4,3,2,0:T(8,128)} %bitcast.286, f32[2,256,16,16]{1,3,2,0:T(8,128)S(1)} %copy-done.21), kind=kLoop, calls=%fused_computation.62 | loop fusion | flops 6160384 | bytes 9437184 | tf_op jit(solution)/shard_map/...ab,...b->...a/dot_general | solution.py:30
  854.7 32.1 %reduce-scatter.12.cloned.1.call-done = bf16[256,1024]{1,0:T(8,128)(2,1)} async-done(((bf16[1024,1024]{1,0:T(8,128)(2,1)}), bf16[256,1024]{1,0:T(8,128)(2,1)}) %reduce-scatter.12.cloned.1.call-update) | async-done | bytes 524304 | tf_op jit(solution)/shard_map/reduce_scatter | solution.py:305
  886.8 430.5 %all-reduce.5 = (f32[256]{0:T(256)}, f32[256,256]{1,0:T(8,128)}, f32[256,256]{1,0:T(8,128)}, f32[256,1024]{1,0:T(8,128)}, f32[256,1024]{1,0:T(8,128)}, /*index=5...) all-reduce(f32[256]{0:T(256)S(1)} %get-tuple-element.267, ...), channel_id=1, replica_groups=mesh['ctx'=8,'fsdp'=4] {'ctx'}, use_global_device_ids=true, to_apply=%region_13.14 | all-reduce | flops 2769408 | bytes 16617472 | tf_op jit(solution)/shard_map/psum | solution.py:324
  (315 shorter events, 372.1 us)
Async XLA Ops:
  7.2 28.8 %copy-start.10 = (bf16[1,512,1024]{2,1,0:T(8,128)(2,1)S(1)}, bf16[1,512,1024]{2,1,0:T(8,128)(2,1)}, u32[]{:S(2)}) copy-start(bf16[1,512,1024]{2,1,0:T(8,128)(2,1)} %param.16) | copy-start | bytes 3145732
  7.2 28.7 %all-gather.12.cloned.1.call-start = ((), (), s32[]{:S(2)}) async-start(), calls=%async_computation.7 | async-start | bytes 2621440 | tf_op jit(solution)/shard_map/all_gather | solution.py:71
  7.9 81.4 %all-gather.14.cloned.1.call-start = ((), (), s32[]{:S(2)}) async-start(), calls=%async_computation.8 | async-start | bytes 2359296 | tf_op jit(solution)/shard_map/all_gather | solution.py:116
  14.6 35.1 %copy-start.49 = (f32[4,1,256]{2,1,0:T(1,128)}, f32[4,1,256]{2,1,0:T(1,128)S(1)}, u32[]{:S(2)}) copy-start(f32[4,1,256]{2,1,0:T(1,128)S(1)} %convert_element_type.281) | copy-start | bytes 12292
  26.1 23.6 %copy-start.53 = (f32[512]{0:T(512)}, f32[512]{0:T(512)S(1)}, u32[]{:S(2)}) copy-start(f32[512]{0:T(512)S(1)} %get-tuple-element.253) | copy-start | bytes 6148
  28.7 186.7 %all-gather.16.cloned.1.call-start = ((), (), s32[]{:S(2)}) async-start(), calls=%async_computation.9 | async-start | bytes 9437184 | tf_op jit(solution)/shard_map/all_gather | solution.py:117
  39.8 349.7 %all-gather.18.cloned.1.call-start = ((), (), s32[]{:S(2)}) async-start(), calls=%async_computation.10 | async-start | bytes 2621440 | tf_op jit(solution)/shard_map/all_gather | solution.py:72
  40.4 365.2 %all-gather.22.cloned.1.call-start = ((), (), s32[]{:S(2)}) async-start(), calls=%async_computation.12 | async-start | bytes 7045120 | tf_op jit(solution)/shard_map/all_gather | solution.py:75
  41.0 373.1 %all-gather.20.cloned.1.call-start = ((), (), s32[]{:S(2)}) async-start(), calls=%async_computation.11 | async-start | bytes 7045120 | tf_op jit(solution)/shard_map/all_gather | solution.py:74
  41.6 381.1 %all-gather.24.cloned.1.call-start = ((), (), s32[]{:S(2)}) async-start(), calls=%async_computation.13 | async-start | bytes 7045120 | tf_op jit(solution)/shard_map/all_gather | solution.py:76
  42.3 488.4 %all-gather.26.cloned.1.call-start = ((), (), s32[]{:S(2)}) async-start(), calls=%async_computation.14 | async-start | bytes 2359296 | tf_op jit(solution)/shard_map/all_gather | solution.py:216
  51.7 549.8 %all-gather.28.cloned.1.call-start = ((), (), s32[]{:S(2)}) async-start(), calls=%async_computation.15 | async-start | bytes 10616832 | tf_op jit(solution)/shard_map/all_gather | solution.py:218
  257.3 111.0 %copy-start.59 = (bf16[273]{0:T(512)(128)(2,1)S(1)}, bf16[273]{0:T(512)(128)(2,1)}, u32[]{:S(2)}) copy-start(bf16[273]{0:T(512)(128)(2,1)} %pad.11.clone) | copy-start | bytes 1642
  464.4 372.2 %reduce-scatter.8.cloned.1.call-start = ((), (), s32[]{:S(2)}) async-start(), calls=%async_computation.16 | async-start | bytes 655360 | tf_op jit(solution)/shard_map/reduce_scatter | solution.py:299
  507.1 329.5 %reduce-scatter.14.cloned.1.call-start = ((), (), s32[]{:S(2)}) async-start(), calls=%async_computation.19 | async-start | bytes 2621440 | tf_op jit(solution)/shard_map/reduce_scatter | solution.py:308
  509.8 326.8 %reduce-scatter.20.cloned.1.call-start = ((), (), s32[]{:S(2)}) async-start(), calls=%async_computation.22 | async-start | bytes 7045120 | tf_op jit(solution)/shard_map/reduce_scatter | solution.py:320
  517.4 319.2 %reduce-scatter.18.cloned.1.call-start = ((), (), s32[]{:S(2)}) async-start(), calls=%async_computation.21 | async-start | bytes 7045120 | tf_op jit(solution)/shard_map/reduce_scatter | solution.py:317
  525.7 311.0 %reduce-scatter.16.cloned.1.call-start = ((), (), s32[]{:S(2)}) async-start(), calls=%async_computation.20 | async-start | bytes 7045120 | tf_op jit(solution)/shard_map/reduce_scatter | solution.py:314
  543.5 311.2 %reduce-scatter.10.cloned.1.call-start = ((), (), s32[]{:S(2)}) async-start(), calls=%async_computation.17 | async-start | bytes 655360 | tf_op jit(solution)/shard_map/reduce_scatter | solution.py:302
  636.0 19.4 %copy-start.44 = (s32[2]{0:T(128)S(1)}, s32[2]{0:T(128)}, u32[]{:S(2)}) copy-start(s32[2]{0:T(128)} %copy-done.43) | copy-start | bytes 28
  636.0 19.4 %copy-start.65 = (s32[2,8]{1,0:T(2,128)S(1)}, s32[2,8]{1,0:T(2,128)}, u32[]{:S(2)}) copy-start(s32[2,8]{1,0:T(2,128)} %copy-done.64) | copy-start | bytes 196
  782.2 18.2 %copy-start.27 = (bf16[2,256,16,16]{1,0,3,2:T(2,128)(2,1)S(1)}, bf16[2,256,16,16]{1,0,3,2:T(2,128)(2,1)}, u32[]{:S(2)}) copy-start(bf16[2,256,16,16]{1,0,3,2:T(2,128)(2,1)} %copy-done.26) | copy-start | bytes 786436
  813.5 73.3 %reduce-scatter.12.cloned.1.call-start = ((), (), s32[]{:S(2)}) async-start(), calls=%async_computation.18 | async-start | bytes 2621440 | tf_op jit(solution)/shard_map/reduce_scatter | solution.py:305
  844.2 42.6 %copy-start.46 = (bf16[256,256]{1,0:T(8,128)(2,1)S(1)}, bf16[256,256]{1,0:T(8,128)(2,1)}, u32[]{:S(2)}) copy-start(bf16[256,256]{1,0:T(8,128)(2,1)} %reduce-scatter.8.cloned.1.call-done) | copy-start | bytes 393220
  (64 other events, 371.1 us)
Sparse Core Ops, SparseCore 0:
  9.6 26.2 all-gather.11
  38.6 50.6 all-gather.13
  92.0 123.4 all-gather.15
  216.9 20.7 all-gather.17
  239.1 43.3 all-gather.21
  283.9 43.3 all-gather.19
  328.9 42.6 all-gather.23
  373.7 49.2 all-gather.25
  464.5 136.9 all-gather.27
  603.9 19.8 reduce-scatter.7
  626.4 31.4 reduce-scatter.13
  660.3 53.9 reduce-scatter.19
  717.1 53.9 reduce-scatter.17
  773.5 54.0 reduce-scatter.15
  830.6 21.7 reduce-scatter.9
  855.4 31.3 reduce-scatter.11
